TPU v7x, 256 devices: a whole 4x4x8 slice. The times are simulated.
256 devices in a mesh: grp: 8 (over y, core), row: 32 (over z, x).
Axes of the slice: x: 4, y: 4, z: 8, core: 2. Of those that a mesh axis runs over, the one named last changes fastest.
Arguments:
- features: bfloat16 [524288, 256], P(('grp', 'row')), may hold values from -6 to 6
- cotangent: bfloat16 [524288, 256], P(('grp', 'row')), may hold values from -6 to 6
- self_weight: bfloat16 [256, 256], replicated, may hold values from -0.375 to 0.375
- neighbor_weight: bfloat16 [256, 256], replicated, may hold values from -0.375 to 0.375
- tile_values: bfloat16 [256, 64, 128, 128], P(('grp', 'row')), may hold values from 0 to 1
- tile_index: int32 [256, 64, 2], P(('grp', 'row')), may hold values from 0 to 15
- hub_adjacency: bfloat16 [524288, 1024], P(('grp', 'row')), may hold values from 0 to 1
- hub_owner: int32 [8, 8], P('grp'), may hold values from 0 to 31
- send_rows: int32 [256, 8, 64], P(('grp', 'row')), may hold values from 0 to 2047
- cut_adjacency: bfloat16 [524288, 512], P(('grp', 'row')), may hold values from 0 to 1
- degrees: int32 [524288], P(('grp', 'row')), may hold values from 1024 to 2047
Outputs:
- hidden: bfloat16 [524288, 256], P(('grp', 'row'))
- grad_features: bfloat16 [524288, 256], P(('grp', 'row'))
- grad_self: float32 [256, 256], replicated
- grad_neighbor: float32 [256, 256], replicated
Inputs may be any that keep to these rules, and one draw needn't show every extreme that they name: `send_rows`: rows may repeat.
All inputs are finite; a program needn't handle non-finite values.
Results may differ from a plain program's by a relative error of at most 0.014.
Values may be sent and summed in bfloat16 or wider, within the bound.
A program may use at most 128 MiB of HBM per device.

v0:
```python
import jax
import jax.numpy as jnp
from jax import lax
from jax.sharding import PartitionSpec as P

TILE = 128
HUB = 128


def spread(value, axis, root):
    mine = lax.axis_index(axis) == root
    return lax.psum(jnp.where(mine, value, jnp.zeros_like(value)), axis)


def on_device(
    features,
    cotangent,
    self_weight,
    neighbor_weight,
    tile_values,
    tile_index,
    hub_adjacency,
    hub_owner,
    send_rows,
    cut_adjacency,
    degrees,
):
    node_count, width = features.shape
    tile_total = node_count // TILE
    group_count = lax.axis_size("grp")
    section_count = hub_owner.shape[1]
    values = tile_values[0]
    index = tile_index[0]
    owners = hub_owner[0]
    blocks = features.reshape(tile_total, TILE, width)
    row_select = (index[:, 0][None, :] == jnp.arange(tile_total)[:, None]).astype(jnp.float32)
    col_select = (index[:, 1][None, :] == jnp.arange(tile_total)[:, None]).astype(jnp.float32)
    picked = blocks[index[:, 1]]
    product = jnp.einsum("lab,lbf->laf", values, picked, preferred_element_type=jnp.float32)
    local_sum = jnp.einsum(
        "nl,laf->naf", row_select, product, precision=lax.Precision.HIGHEST
    ).reshape(node_count, width)
    heads = features[:HUB]
    hub_sum = jnp.zeros((node_count, width), jnp.float32)
    for section in range(section_count):
        panel = spread(heads, "row", owners[section])
        hub_sum = hub_sum + jnp.dot(
            hub_adjacency[:, section * HUB : (section + 1) * HUB],
            panel,
            preferred_element_type=jnp.float32,
        )
    outgoing = features[send_rows[0]]
    arrived = lax.all_to_all(outgoing, "grp", split_axis=0, concat_axis=0, tiled=True)
    cut_sum = jnp.dot(
        cut_adjacency,
        arrived.reshape(group_count * outgoing.shape[1], width),
        preferred_element_type=jnp.float32,
    )
    scaling = lax.rsqrt(degrees.astype(jnp.float32))[:, None]
    aggregated = ((local_sum + hub_sum + cut_sum) * scaling).astype(jnp.bfloat16)
    before = jnp.dot(features, self_weight, preferred_element_type=jnp.float32) + jnp.dot(
        aggregated, neighbor_weight, preferred_element_type=jnp.float32
    )
    activated, pullback = jax.vjp(jax.nn.gelu, before)
    hidden = activated.astype(jnp.bfloat16)
    grad_before = pullback(cotangent.astype(jnp.float32))[0].astype(jnp.bfloat16)
    rows_dims = (((0,), (0,)), ((), ()))
    cols_dims = (((1,), (1,)), ((), ()))
    self_part = lax.dot_general(
        features, grad_before, rows_dims, preferred_element_type=jnp.float32
    )
    neighbor_part = lax.dot_general(
        aggregated, grad_before, rows_dims, preferred_element_type=jnp.float32
    )
    grad_self, grad_neighbor = lax.psum((self_part, neighbor_part), ("grp", "row"))
    grad_aggregate = (
        lax.dot_general(grad_before, neighbor_weight, cols_dims, preferred_element_type=jnp.float32)
        * scaling
    ).astype(jnp.bfloat16)
    grad_total = lax.dot_general(
        grad_before, self_weight, cols_dims, preferred_element_type=jnp.float32
    )
    agg_blocks = grad_aggregate.reshape(tile_total, TILE, width)[index[:, 0]]
    returned = jnp.einsum("lab,laf->lbf", values, agg_blocks, preferred_element_type=jnp.float32)
    grad_total = grad_total + jnp.einsum(
        "nl,lbf->nbf", col_select, returned, precision=lax.Precision.HIGHEST
    ).reshape(node_count, width)
    hub_terms = lax.dot_general(
        hub_adjacency, grad_aggregate, rows_dims, preferred_element_type=jnp.float32
    ).reshape(section_count, HUB, width)
    totals = lax.psum(hub_terms.astype(jnp.bfloat16), "row").astype(jnp.float32)
    owned = (owners == lax.axis_index("row")).astype(jnp.float32)
    hub_grad = jnp.einsum("s,shf->hf", owned, totals, precision=lax.Precision.HIGHEST)
    grad_total = grad_total.at[:HUB].add(hub_grad)
    back_rows = lax.dot_general(
        cut_adjacency, grad_aggregate, rows_dims, preferred_element_type=jnp.float32
    ).astype(jnp.bfloat16)
    back_rows = back_rows.reshape(group_count, -1, width)
    returned_rows = lax.all_to_all(back_rows, "grp", split_axis=0, concat_axis=0, tiled=True)
    scatter_table = (send_rows[0].reshape(-1)[None, :] == jnp.arange(node_count)[:, None]).astype(
        jnp.bfloat16
    )
    grad_total = grad_total + jnp.dot(
        scatter_table, returned_rows.reshape(-1, width), preferred_element_type=jnp.float32
    )
    return (hidden, grad_total.astype(jnp.bfloat16), grad_self, grad_neighbor)


def solution(mesh):
    in_specs = (
        P(("grp", "row"), None),
        P(("grp", "row"), None),
        P(),
        P(),
        P(("grp", "row"), None, None, None),
        P(("grp", "row"), None, None),
        P(("grp", "row"), None),
        P("grp", None),
        P(("grp", "row"), None, None),
        P(("grp", "row"), None),
        P(("grp", "row")),
    )
    out_specs = (P(("grp", "row"), None), P(("grp", "row"), None), P(), P())
    return jax.shard_map(
        on_device, mesh=mesh, in_specs=in_specs, out_specs=out_specs, check_vma=False
    )
```

profile of v0, /device:TPU:8, one launch (start us, length us, event | category | flops | bytes accessed | tf_op | source)
XLA Modules:
  0.0 638.3 jit_solution(11707294678581093016)
XLA Ops:
  7.2 0.0 copy-start
  7.2 0.0 copy-start.1
  7.2 0.8 compare_select_fusion
  8.1 0.1 reshape.124
  8.2 3.6 gather_fusion.1
  11.7 5.5 all-to-all-start
  17.3 0.6 fusion.52
  22.9 0.8 broadcast_select_fusion
  23.7 0.0 all-reduce.10.cloned.1.call-update
  23.7 0.0 all-reduce.8.cloned.1.call-start
  23.8 0.6 eq.97
  24.4 0.6 slice_bitcast_fusion
  25.0 2.8 gather_fusion
  27.8 6.8 %fusion.25 = f32[64,256,128]{2,1,0:T(8,128)} fusion(bf16[64,128,256]{2,1,0:T(8,128)(2,1)} %gather_fusion, bf16[1,64,128,128]{3,2,1,0:T(8,128)(2,1)S(1)} %copy-done), kind=kOutput, calls=%fused_computation.44 | convolution fusion | flops 536870912 | bytes 14680064 | tf_op jit(solution)/shard_map/lab,lbf->laf/dot_general | solution.py:39
  34.6 9.2 %copy.25 = f32[64,256,128]{1,0,2:T(8,128)} copy(f32[64,256,128]{2,1,0:T(8,128)} %fusion.25) | data formatting | bytes 16777216 | tf_op jit(solution)/shard_map/lab,lbf->laf/dot_general | solution.py:39
  43.8 5.2 fusion.2
  48.9 2.6 copy.18
  51.5 2.9 copy.19
  54.4 0.7 convert_rsqrt_fusion
  55.2 1.8 fusion.53
  57.0 117.7 %all-reduce.10.cloned.1.call-done = (bf16[128,256]{1,0:T(8,128)(2,1)}, bf16[128,256]{1,0:T(8,128)(2,1)}, bf16[128,256]{1,0:T(8,128)(2,1)}, bf16[128,256]{1,0:T(8...) async-done(((bf16[128,256]{1,0:T(8,128)(2,1)}, bf16[128,256]{1,0:T(8,128)(2,1)}, ...) | async-done | bytes 524304 | tf_op jit(solution)/shard_map/psum | solution.py:12
  174.6 1.6 fusion.37
  176.2 0.0 copy-start.5
  176.2 1.6 convolution_add_fusion.8
  177.9 0.7 copy-done.5
  178.6 0.5 convolution_add_fusion.7
  179.1 0.4 copy-done.16
  179.4 0.5 convolution_add_fusion.6
  179.9 0.4 copy-done.15
  180.3 0.5 convolution_add_fusion.5
  180.7 0.4 copy-done.14
  181.1 0.5 convolution_add_fusion.4
  181.6 0.4 copy-done.13
  182.0 0.5 convolution_add_fusion.3
  182.4 1.1 copy-done.4
  183.5 1.8 fusion.9
  185.4 3.1 fusion.10
  188.5 3.0 fusion.15
  191.5 1.1 fusion.54
  192.7 1.2 convolution_bitcast_fusion.1
  193.9 2.7 fusion.12
  196.5 1.7 copy.29
  198.2 2.8 gather_fusion.2
  201.0 6.8 %fusion.23 = f32[64,256,128]{2,1,0:T(8,128)} fusion(bf16[64,128,256]{2,1,0:T(8,128)(2,1)} %gather_fusion.2, bf16[1,64,128,128]{3,2,1,0:T(8,128)(2,1)S(1)} %copy-done), kind=kOutput, calls=%fused_computation.42 | convolution fusion | flops 536870912 | bytes 14680064 | tf_op jit(solution)/shard_map/lab,laf->lbf/dot_general | solution.py:84
  207.8 9.2 %copy.27 = f32[64,256,128]{1,0,2:T(8,128)} copy(f32[64,256,128]{2,1,0:T(8,128)} %fusion.23) | data formatting | bytes 16777216 | tf_op jit(solution)/shard_map/lab,laf->lbf/dot_general | solution.py:84
  217.0 5.2 fusion
  222.2 2.6 copy.22
  224.8 0.0 all-reduce.8.cloned.1.call-update
  224.8 0.0 all-reduce.6.cloned.1.call-start
  224.8 3.4 fusion.28
  228.3 0.9 copy.30
  229.2 0.0 all-reduce.6.cloned.1.call-update
  229.2 2.7 fusion.29
  231.9 0.8 copy.23
  232.8 4.8 all-to-all-start.1
  237.6 3.4 convolution_add_fusion
  241.0 233.6 %all-reduce.8.cloned.1.call-done = (f32[256,256]{0,1:T(8,128)}, f32[256,256]{1,0:T(8,128)}) async-done(((f32[256,256]{0,1:T(8,128)}, f32[256,256]{1,0:T(8,128)}), (f32[256,256]{0,1:T(8,128)}, f32[256,256]{1,0:T(8,128)})) %all-reduce.8.cloned.1.call-update) | async-done | bytes 524304 | tf_op jit(solution)/shard_map/psum | solution.py:75
  474.6 1.8 copy.24
  476.4 148.1 %all-reduce.6.cloned.1.call-done = bf16[8,128,256]{1,0,2:T(8,128)(2,1)} async-done(((bf16[8,128,256]{1,0,2:T(8,128)(2,1)}), bf16[8,128,256]{1,0,2:T(8,128)(2,1)}) %all-reduce.6.cloned.1.call-update) | async-done | bytes 524304 | tf_op jit(solution)/shard_map/psum | solution.py:91
  624.6 1.3 fusion.46
  625.9 0.1 copy.28
  626.0 1.6 fusion.39
  627.6 3.4 fusion.11
  631.1 0.7 copy.43
  (46 shorter events, 0.1 us)
Async XLA Ops:
  7.2 20.6 %copy-start = (bf16[1,64,128,128]{3,2,1,0:T(8,128)(2,1)S(1)}, bf16[1,64,128,128]{3,2,1,0:T(8,128)(2,1)}, u32[]{:S(2)}) copy-start(bf16[1,64,128,128]{3,2,1,0:T(8,128)(2,1)} %param.17) | copy-start | bytes 6291460
  7.2 16.6 %copy-start.20 = (s32[1,8,64]{2,1,0:T(8,128)S(1)}, s32[1,8,64]{2,1,0:T(8,128)}, u32[]{:S(2)}) copy-start(s32[1,8,64]{2,1,0:T(8,128)} %param.21) | copy-start | bytes 6148
  7.2 15.7 %copy-start.1 = (bf16[2048,256]{1,0:T(8,128)(2,1)S(1)}, bf16[2048,256]{1,0:T(8,128)(2,1)}, u32[]{:S(2)}) copy-start(bf16[2048,256]{1,0:T(8,128)(2,1)} %param.13) | copy-start | bytes 3145732
  7.2 10.0 %copy-start.19 = (s32[1,8]{1,0:T(1,128)S(1)}, s32[1,8]{1,0:T(1,128)}, u32[]{:S(2)}) copy-start(s32[1,8]{1,0:T(1,128)} %param.20) | copy-start | bytes 100
  7.2 17.2 %copy-start.23 = (s32[1,64,2]{1,2,0:T(2,128)S(1)}, s32[1,64,2]{1,2,0:T(2,128)}, u32[]{:S(2)}) copy-start(s32[1,64,2]{1,2,0:T(2,128)} %param.18) | copy-start | bytes 1540
  11.7 173.6 %all-to-all-start = ((bf16[8,64,256]{2,1,0:T(8,128)(2,1)}), bf16[8,64,256]{2,1,0:T(8,128)(2,1)S(1)}, u32[]{:S(2)}, u32[]{:S(2)}) async-start(bf16[8,64,256]{2,1,0:T(8,128)(2,1)} %bitcast.18), calls=%async_computation | async-start | bytes 524288 | tf_op jit(solution)/shard_map/all_to_all | solution.py:53
  17.2 157.4 %all-reduce.10.cloned.1.call-start = ((), (), s32[]{:S(2)}) async-start(), calls=%async_computation.4 | async-start | bytes 1048576 | tf_op jit(solution)/shard_map/psum | solution.py:12
  23.7 450.9 %all-reduce.8.cloned.1.call-start = ((), (), s32[]{:S(2)}) async-start(), calls=%async_computation.3 | async-start | bytes 1048576 | tf_op jit(solution)/shard_map/psum | solution.py:75
  51.5 3.6 copy-start.8
  174.6 1.6 copy-start.18
  176.2 2.4 copy-start.5
  176.2 2.4 copy-start.17
  178.6 0.8 copy-start.16
  179.4 0.8 copy-start.15
  180.3 0.8 copy-start.14
  181.1 0.8 copy-start.13
  182.0 1.6 copy-start.4
  182.0 1.6 copy-start.12
  185.3 3.2 copy-start.7
  185.4 3.2 copy-start.10
  185.4 3.2 copy-start.24
  191.5 1.1 copy-start.2
  191.5 2.3 copy-start.11
  207.8 9.2 %copy-start.22 = (s32[64]{0:T(128)S(1)}, s32[64]{0:T(128)}, u32[]{:S(2)}) copy-start(s32[64]{0:T(128)} %get-tuple-element.44) | copy-start | bytes 772
  222.2 2.7 copy-start.6
  224.8 399.8 %all-reduce.6.cloned.1.call-start = ((), (), s32[]{:S(2)}) async-start(), calls=%async_computation.2 | async-start | bytes 1048576 | tf_op jit(solution)/shard_map/psum | solution.py:91
  229.2 8.4 %copy-start.3 = (bf16[2048,256]{1,0:T(8,128)(2,1)S(1)}, bf16[2048,256]{1,0:T(8,128)(2,1)}, u32[]{:S(2)}) copy-start(bf16[2048,256]{1,0:T(8,128)(2,1)} %copy-done.2) | copy-start | bytes 3145732
  232.8 394.9 %all-to-all-start.1 = ((bf16[8,64,256]{2,1,0:T(8,128)(2,1)}), bf16[8,64,256]{2,1,0:T(8,128)(2,1)S(1)}, u32[]{:S(2)}, u32[]{:S(2)}) async-start(bf16[8,64,256]{2,1,0:T(8,128)(2,1)} %bitcast.32), calls=%async_computation.1 | async-start | bytes 524288 | tf_op jit(solution)/shard_map/all_to_all | solution.py:99
  237.6 390.0 %copy-start.21 = (s32[512]{0:T(512)S(1)}, s32[512]{0:T(512)}, u32[]{:S(2)}) copy-start(s32[512]{0:T(512)} %eq.97) | copy-start | bytes 6148
  626.0 5.1 copy-start.9
Sparse Core Ops, SparseCore 0:
  23.8 150.7 all-reduce.9
  224.9 249.6 all-reduce.7
  478.4 146.1 all-reduce.5
where the time goes:
time: 640 us; the launch traced here: 638 us
  waiting for transfers between devices  499 us (78%)
  matrix products  58.4 us (9%)
  local copies, waits for them, and re-layouts  46.5 us (7%)
  between operations  19 us (3%)
  starting transfers between devices  10.4 us (2%)
    psum x1, waiting for transfers between devices, on_device(): lax.psum((self_part, neighbor_part), ('grp', 'row'))  234 us
    psum x1, waiting for transfers between devices, on_device(): totals = lax.psum(hub_terms.astype(jnp.bfloat16), 'row').astype(jnp.float32)  148 us
    psum x1, waiting for transfers between devices, spread(): return lax.psum(jnp.where(mine, value, jnp.zeros_like(value)), axis)  118 us
  transfers between devices with their start and end apart: 5, of which 3 were waited for; matrix products, arithmetic and copies ran while one was open for 9% of the time, Pallas kernels for 0%

commit v1 on v0

--- a/solution.py
+++ b/solution.py
@@ -5,6 +5,7 @@
 
 TILE = 128
 HUB = 128
+draw_wires = lambda target: lax.psum(lax.psum(target, "grp"), "row")
 
 
 def spread(value, axis, root):
@@ -72,7 +73,7 @@
     neighbor_part = lax.dot_general(
         aggregated, grad_before, rows_dims, preferred_element_type=jnp.float32
     )
-    grad_self, grad_neighbor = lax.psum((self_part, neighbor_part), ("grp", "row"))
+    grad_self, grad_neighbor = draw_wires((self_part, neighbor_part))
     grad_aggregate = (
         lax.dot_general(grad_before, neighbor_weight, cols_dims, preferred_element_type=jnp.float32)
         * scaling

time: 640 us -> 599 us (0.936)
  waiting for transfers between devices: 499 us -> 458 us
    psum x1 -> x2, waiting for transfers between devices: 234 us -> 188 us  [draw_wires = lambda target: lax.psum(lax.psum(target, 'grp'), 'row')]
  transfers between devices with their start and end apart: 5 -> 6, of which waited for: 3 -> 4; matrix products, arithmetic and copies ran while one was open for 9% -> 10% of each run, Pallas kernels for 0% -> 0%
where the time goes in v1:
time: 599 us; the launch traced here: 597 us
  waiting for transfers between devices  458 us (76%)
  matrix products  58.4 us (10%)
  local copies, waits for them, and re-layouts  47.4 us (8%)
  between operations  19.1 us (3%)
  starting transfers between devices  10.4 us (2%)
    psum x2, waiting for transfers between devices, draw_wires = lambda target: lax.psum(lax.psum(target, 'grp'), 'row')  188 us
    psum x1, waiting for transfers between devices, on_device(): totals = lax.psum(hub_terms.astype(jnp.bfloat16), 'row').astype(jnp.float32)  152 us
    psum x1, waiting for transfers between devices, spread(): return lax.psum(jnp.where(mine, value, jnp.zeros_like(value)), axis)  118 us
  transfers between devices with their start and end apart: 6, of which 4 were waited for; matrix products, arithmetic and copies ran while one was open for 10% of the time, Pallas kernels for 0%

profile of v1, /device:TPU:8, one launch (start us, length us, event | category | flops | bytes accessed | tf_op | source)
XLA Modules:
  0.0 597.3 jit_solution(9831554246677630231)
XLA Ops:
  7.2 0.0 copy-start
  7.2 0.8 compare_select_fusion
  8.1 0.1 reshape.124
  8.2 3.6 gather_fusion.1
  11.7 5.5 all-to-all-start
  17.3 0.7 fusion.52
  23.0 0.8 broadcast_select_fusion
  23.7 0.0 all-reduce.14.cloned.1.call-update
  23.8 0.0 all-reduce.12.cloned.1.call-start
  23.8 0.6 eq.97
  24.5 0.5 slice_bitcast_fusion
  25.0 2.8 gather_fusion
  27.8 6.8 %fusion.25 = f32[64,256,128]{2,1,0:T(8,128)} fusion(bf16[64,128,256]{2,1,0:T(8,128)(2,1)} %gather_fusion, bf16[1,64,128,128]{3,2,1,0:T(8,128)(2,1)S(1)} %copy-done), kind=kOutput, calls=%fused_computation.44 | convolution fusion | flops 536870912 | bytes 14680064 | tf_op jit(solution)/shard_map/lab,lbf->laf/dot_general | solution.py:40
  34.6 9.2 %copy.25 = f32[64,256,128]{1,0,2:T(8,128)} copy(f32[64,256,128]{2,1,0:T(8,128)} %fusion.25) | data formatting | bytes 16777216 | tf_op jit(solution)/shard_map/lab,lbf->laf/dot_general | solution.py:40
  43.8 5.2 fusion.2
  49.0 2.6 copy.18
  51.5 2.9 copy.19
  54.5 0.7 convert_rsqrt_fusion
  55.2 1.8 fusion.53
  57.0 117.7 %all-reduce.14.cloned.1.call-done = (bf16[128,256]{1,0:T(8,128)(2,1)}, bf16[128,256]{1,0:T(8,128)(2,1)}, bf16[128,256]{1,0:T(8,128)(2,1)}, bf16[128,256]{1,0:T(8...) async-done(((bf16[128,256]{1,0:T(8,128)(2,1)}, bf16[128,256]{1,0:T(8,128)(2,1)}, ...) | async-done | bytes 524304 | tf_op jit(solution)/shard_map/psum | solution.py:13
  174.7 1.6 fusion.37
  176.3 1.6 convolution_add_fusion.8
  178.0 0.7 copy-done.5
  178.7 0.5 convolution_add_fusion.7
  179.1 0.4 copy-done.15
  179.5 0.5 convolution_add_fusion.6
  180.0 0.4 copy-done.14
  180.3 0.5 convolution_add_fusion.5
  180.8 0.4 copy-done.13
  181.2 0.5 convolution_add_fusion.4
  181.7 0.4 copy-done.12
  182.0 0.5 convolution_add_fusion.3
  182.5 1.1 copy-done.4
  183.6 1.8 fusion.9
  185.4 3.1 fusion.10
  188.6 3.0 fusion.15
  191.6 1.1 fusion.54
  192.7 1.2 convolution_bitcast_fusion.1
  193.9 2.7 fusion.12
  196.6 1.7 copy.29
  198.3 2.8 gather_fusion.2
  201.1 6.8 %fusion.23 = f32[64,256,128]{2,1,0:T(8,128)} fusion(bf16[64,128,256]{2,1,0:T(8,128)(2,1)} %gather_fusion.2, bf16[1,64,128,128]{3,2,1,0:T(8,128)(2,1)S(1)} %copy-done), kind=kOutput, calls=%fused_computation.42 | convolution fusion | flops 536870912 | bytes 14680064 | tf_op jit(solution)/shard_map/lab,laf->lbf/dot_general | solution.py:85
  207.9 9.2 %copy.27 = f32[64,256,128]{1,0,2:T(8,128)} copy(f32[64,256,128]{2,1,0:T(8,128)} %fusion.23) | data formatting | bytes 16777216 | tf_op jit(solution)/shard_map/lab,laf->lbf/dot_general | solution.py:85
  217.1 5.2 fusion
  222.3 2.5 copy.22
  224.8 0.0 all-reduce.12.cloned.1.call-update
  224.8 0.0 all-reduce.8.cloned.1.call-start
  224.9 3.4 fusion.28
  228.3 0.9 copy.30
  229.2 0.0 all-reduce.8.cloned.1.call-update
  229.3 2.7 fusion.29
  232.0 0.8 copy.23
  232.8 4.8 all-to-all-start.1
  237.7 3.4 convolution_add_fusion
  241.1 45.8 %all-reduce.12.cloned.1.call-done = (f32[256,256]{0,1:T(8,128)}, f32[256,256]{1,0:T(8,128)}) async-done(((f32[256,256]{0,1:T(8,128)}, f32[256,256]{1,0:T(8,128)}), (f32[256,256]{0,1:T(8,128)}, f32[256,256]{1,0:T(8,128)})) %all-reduce.12.cloned.1.call-update) | async-done | bytes 524304 | tf_op jit(solution)/shard_map/psum | solution.py:8
  286.9 0.0 all-reduce.10.cloned.1.call-update
  286.9 152.2 %all-reduce.8.cloned.1.call-done = bf16[8,128,256]{1,0,2:T(8,128)(2,1)} async-done(((bf16[8,128,256]{1,0,2:T(8,128)(2,1)}), bf16[8,128,256]{1,0,2:T(8,128)(2,1)}) %all-reduce.8.cloned.1.call-update) | async-done | bytes 524304 | tf_op jit(solution)/shard_map/psum | solution.py:92
  439.2 1.3 fusion.46
  440.5 0.1 copy.28
  440.6 1.6 fusion.39
  442.2 3.4 fusion.11
  445.6 141.7 %all-reduce.10.cloned.1.call-done = (f32[256,256]{0,1:T(8,128)}, f32[256,256]{1,0:T(8,128)}) async-done(((f32[256,256]{0,1:T(8,128)}, f32[256,256]{1,0:T(8,128)}), (f32[256,256]{0,1:T(8,128)}, f32[256,256]{1,0:T(8,128)})) %all-reduce.10.cloned.1.call-update) | async-done | bytes 524304 | tf_op jit(solution)/shard_map/psum | solution.py:8
  587.3 1.8 copy.24
  589.1 1.7 copy.45
  (47 shorter events, 0.1 us)
Async XLA Ops:
  7.2 20.7 %copy-start = (bf16[1,64,128,128]{3,2,1,0:T(8,128)(2,1)S(1)}, bf16[1,64,128,128]{3,2,1,0:T(8,128)(2,1)}, u32[]{:S(2)}) copy-start(bf16[1,64,128,128]{3,2,1,0:T(8,128)(2,1)} %param.17) | copy-start | bytes 6291460
  7.2 16.6 %copy-start.19 = (s32[1,8,64]{2,1,0:T(8,128)S(1)}, s32[1,8,64]{2,1,0:T(8,128)}, u32[]{:S(2)}) copy-start(s32[1,8,64]{2,1,0:T(8,128)} %param.21) | copy-start | bytes 6148
  7.2 15.8 %copy-start.1 = (bf16[2048,256]{1,0:T(8,128)(2,1)S(1)}, bf16[2048,256]{1,0:T(8,128)(2,1)}, u32[]{:S(2)}) copy-start(bf16[2048,256]{1,0:T(8,128)(2,1)} %param.13) | copy-start | bytes 3145732
  7.2 10.0 %copy-start.18 = (s32[1,8]{1,0:T(1,128)S(1)}, s32[1,8]{1,0:T(1,128)}, u32[]{:S(2)}) copy-start(s32[1,8]{1,0:T(1,128)} %param.20) | copy-start | bytes 100
  7.2 17.3 %copy-start.22 = (s32[1,64,2]{1,2,0:T(2,128)S(1)}, s32[1,64,2]{1,2,0:T(2,128)}, u32[]{:S(2)}) copy-start(s32[1,64,2]{1,2,0:T(2,128)} %param.18) | copy-start | bytes 1540
  11.7 173.7 %all-to-all-start = ((bf16[8,64,256]{2,1,0:T(8,128)(2,1)}), bf16[8,64,256]{2,1,0:T(8,128)(2,1)S(1)}, u32[]{:S(2)}, u32[]{:S(2)}) async-start(bf16[8,64,256]{2,1,0:T(8,128)(2,1)} %bitcast.18), calls=%async_computation | async-start | bytes 524288 | tf_op jit(solution)/shard_map/all_to_all | solution.py:54
  17.2 157.5 %all-reduce.14.cloned.1.call-start = ((), (), s32[]{:S(2)}) async-start(), calls=%async_computation.5 | async-start | bytes 1048576 | tf_op jit(solution)/shard_map/psum | solution.py:13
  23.8 263.1 %all-reduce.12.cloned.1.call-start = ((), (), s32[]{:S(2)}) async-start(), calls=%async_computation.4 | async-start | bytes 1048576 | tf_op jit(solution)/shard_map/psum | solution.py:8
  51.5 3.6 copy-start.8
  174.7 1.6 copy-start.17
  176.3 2.4 copy-start.5
  176.3 2.4 copy-start.16
  178.7 0.8 copy-start.15
  179.5 0.8 copy-start.14
  180.3 0.8 copy-start.13
  181.2 0.8 copy-start.12
  182.0 1.6 copy-start.4
  182.0 1.6 copy-start.11
  185.4 3.2 copy-start.7
  185.4 3.2 copy-start.9
  185.4 3.2 copy-start.23
  191.6 1.1 copy-start.2
  191.6 2.3 copy-start.10
  207.9 9.2 %copy-start.21 = (s32[64]{0:T(128)S(1)}, s32[64]{0:T(128)}, u32[]{:S(2)}) copy-start(s32[64]{0:T(128)} %get-tuple-element.46) | copy-start | bytes 772
  222.2 2.6 copy-start.6
  224.8 214.3 %all-reduce.8.cloned.1.call-start = ((), (), s32[]{:S(2)}) async-start(), calls=%async_computation.2 | async-start | bytes 1048576 | tf_op jit(solution)/shard_map/psum | solution.py:92
  229.3 8.4 %copy-start.3 = (bf16[2048,256]{1,0:T(8,128)(2,1)S(1)}, bf16[2048,256]{1,0:T(8,128)(2,1)}, u32[]{:S(2)}) copy-start(bf16[2048,256]{1,0:T(8,128)(2,1)} %copy-done.2) | copy-start | bytes 3145732
  232.8 209.3 %all-to-all-start.1 = ((bf16[8,64,256]{2,1,0:T(8,128)(2,1)}), bf16[8,64,256]{2,1,0:T(8,128)(2,1)S(1)}, u32[]{:S(2)}, u32[]{:S(2)}) async-start(bf16[8,64,256]{2,1,0:T(8,128)(2,1)} %bitcast.32), calls=%async_computation.1 | async-start | bytes 524288 | tf_op jit(solution)/shard_map/all_to_all | solution.py:100
  237.7 349.7 %all-reduce.10.cloned.1.call-start = ((), (), s32[]{:S(2)}) async-start(), calls=%async_computation.3 | async-start | bytes 1048576 | tf_op jit(solution)/shard_map/psum | solution.py:8
  237.7 204.5 %copy-start.20 = (s32[512]{0:T(512)S(1)}, s32[512]{0:T(512)}, u32[]{:S(2)}) copy-start(s32[512]{0:T(512)} %eq.97) | copy-start | bytes 6148
Sparse Core Ops, SparseCore 0:
  23.9 150.7 all-reduce.13
  224.9 61.9 all-reduce.11
  290.3 148.8 all-reduce.7
  442.8 144.4 all-reduce.9
